TPU v7x, 32 devices: a whole 2x2x4 slice. The times are simulated.
32 devices in a mesh: grp: 2 (over x), facet: 16 (over z, y, core).
Axes of the slice: x: 2, y: 2, z: 4, core: 2. Of those that a mesh axis runs over, the one named last changes fastest.
Arguments:
- image: float32 [16, 256, 256], P(None, 'facet', 'grp'), may hold values from 0 to 2
- wavelet_dual: bfloat16 [8, 16, 256, 256], P(None, None, 'facet', 'grp'), may hold values from -6 to 6
- thresholds: float32 [8, 256, 256], P(None, 'facet', 'grp'), may hold values from 1 to 10
- filter_taps: float32 [8, 2, 7], replicated, may hold values from -2 to 2
- visibilities: float32 [16, 2, 8, 16, 256], P('facet', 'grp'), may hold values from -6 to 6
- data_dual: float32 [16, 2, 8, 16, 256], P('facet', 'grp'), may hold values from -6 to 6
- ball_radii: float32 [16, 2, 8], P('facet', 'grp'), may hold values from 19.2 to 256
- blocks: bfloat16 [16, 2, 16, 256, 256], P('facet', 'grp'), may hold values from -0.375 to 0.375
- row_index: int32 [16, 2, 16], P('facet', 'grp'), may hold values from 0 to 7
- col_index: int32 [16, 2, 16], P('facet', 'grp'), may hold values from 0 to 23
Outputs:
- image_out: float32 [16, 256, 256], P(None, 'facet', 'grp')
- data_dual_out: float32 [16, 2, 8, 16, 256], P('facet', 'grp')
- wavelet_dual_out: bfloat16 [8, 16, 256, 256], P(None, None, 'facet', 'grp')
Inputs may be any that keep to these rules, and one draw needn't show every extreme that they name: `row_index`: the visibility block of the same device that an operator block feeds. `col_index`: a tile of the band of three facets (the facet above, the device's own, the facet below) over the device's 128 columns, numbered row of tiles by row of tiles, 8 tiles a row.
All inputs are finite; a program needn't handle non-finite values.
Results may differ from a plain program's by a relative error of at most 0.0071.
Values may be sent and summed in bfloat16 or wider, within the bound.
A program may use at most 64 MiB of HBM per device.

v0:
```python
import functools

import jax
import jax.numpy as jnp
from jax import lax
from jax.experimental import pallas as pl
from jax.experimental.pallas import tpu as pltpu
from jax.sharding import PartitionSpec as P

W = 3
TS = 16
ITERS = 2
MESH = pl.DeviceIdType.MESH
F32 = jnp.float32
BF16 = jnp.bfloat16
ROWS = ((-1, 0), (1, 0))
SIDES = ((0, -1), (0, 1), (-1, -1), (-1, 1), (1, -1), (1, 1))
DIRS = ROWS + SIDES
ROW_SLOT = {0: 0, 1: 1, -1: 2}
SIDE_SLOT = {1: 0, -1: 1}


def iota(shape, dim):
    return lax.broadcasted_iota(jnp.int32, shape, dim)


def tap_matrix(position, taps):
    out = jnp.zeros(position.shape, F32)
    for tap, value in enumerate(taps):
        out = jnp.where(position == tap, value, out)
    return out


def swap_groups(items):
    count = len(items)
    lanes = items[0].shape[-1]
    group = iota(items[0].shape, 1) // TS
    step = count // 2
    while step:
        low = (group // step) % 2 == 0
        out = list(items)
        for a in range(count):
            if (a // step) % 2 == 0:
                first, second = items[a], items[a + step]
                out[a] = jnp.where(low, first, pltpu.roll(second, step * TS, 1))
                out[a + step] = jnp.where(low, pltpu.roll(first, lanes - step * TS, 1), second)
        items = out
        step //= 2
    return items


def kernel(
    sizes,
    image, dual_wave, thresholds, taps, seen, dual_data, radius, blocks, row_ids, col_ids,
    image_out, data_out, wave_out,
    u_in, ops, thr, vis, vdat, ttap, stap, rtap, ptap, ycols, rfilt,
    near, zrim, ztile, zedge, zedge_own, rim_own, rim, edge_own, edge, tsum_own, tsum,
    parts, uslot, vslot, xslot, turn,
    local_sem, send_sem, recv_sem,
):
    nf, ng, NB, C, R, L, KB, RB, PIX, VB, TAPS, NT3 = sizes
    f = lax.axis_index("facet")
    g = lax.axis_index("grp")
    T1 = L // TS
    LC = C * L
    EW = L // C

    def exists(d):
        df, dg = d
        ok = None
        for test in ([f > 0] if df < 0 else [f < nf - 1] if df > 0 else []) + (
            [g > 0] if dg < 0 else [g < ng - 1] if dg > 0 else []
        ):
            ok = test if ok is None else jnp.logical_and(ok, test)
        return ok

    def back(d):
        return (-d[0], -d[1])

    def where_to(d):
        return {"facet": f + d[0], "grp": g + d[1]}

    loads = [
        pltpu.make_async_copy(src, dst, local_sem.at[n])
        for n, (src, dst) in enumerate(
            ((dual_wave, u_in), (dual_data, vdat), (blocks, ops), (seen, vis), (thresholds, thr))
        )
    ]
    for load in loads:
        load.start()

    for ref in (rim, edge, tsum, near, zedge):
        ref[...] = jnp.zeros(ref.shape, ref.dtype)
    for it in range(ITERS):
        ztile[it, :T1] = jnp.zeros((T1, C, PIX), BF16)
        ztile[it, 2 * T1 :] = jnp.zeros((T1, C, PIX), BF16)

    barrier = pltpu.get_barrier_semaphore()
    for d in DIRS:
        @pl.when(exists(d))
        def _(d=d):
            pl.semaphore_signal(barrier, inc=1, device_id=where_to(d), device_id_type=MESH)

    src = iota((L, L), 0)
    dst = iota((L, L), 1)
    m_dst = dst % EW
    m_src = src % EW
    over = jnp.where(m_dst < W, m_dst - W, jnp.where(m_dst < 2 * W, L + m_dst - W, 4 * L))
    halo = jnp.where(m_src < W, L + m_src, jnp.where(m_src < 2 * W, m_src - 2 * W, 4 * L))
    row_out = iota((2 * R, NB * R), 0)
    row_out = jnp.where(row_out < R, row_out, jnp.where(row_out < R + W, row_out - R - W, jnp.where(row_out < R + 2 * W, row_out - W, 4 * L)))
    row_in = iota((2 * R, NB * R), 1)
    row_at = iota((R, 3 * R), 1)
    row_at = jnp.where(row_at < R, row_at, jnp.where(row_at < 2 * R, row_at - 2 * R, row_at - R))
    row_to = iota((R, 3 * R), 0)
    synth_rows = jnp.zeros((2 * R, NB * R), F32)
    for b in range(NB):
        rt = [taps[b, 0, t] for t in range(TAPS)]
        ct = [taps[b, 1, t] for t in range(TAPS)]
        ch = [0.5 * t for t in ct]
        stap[b, :, :L] = tap_matrix(dst + W - src, ct).astype(BF16)
        stap[b, :, L:] = tap_matrix(over + W - src, ct).astype(BF16)
        ttap[b, :L] = tap_matrix(src - dst + W, ch).astype(BF16)
        ttap[b, L:] = tap_matrix(halo - dst + W, ch).astype(BF16)
        rtap[b * R : (b + 1) * R] = tap_matrix(row_at - row_to + W, rt).astype(BF16)
        synth_rows = jnp.where(row_in // R == b, tap_matrix(row_out + W - (row_in - b * R), rt), synth_rows)
    ptap[...] = synth_rows.astype(BF16)
    pick = jnp.where(jnp.logical_or(jnp.logical_and(m_dst < W, src == m_dst), jnp.logical_and(jnp.logical_and(m_dst >= W, m_dst < 2 * W), src == L - 2 * W + m_dst)), 1.0, 0.0).astype(BF16)
    place = jnp.where(jnp.logical_or(jnp.logical_and(m_src < W, dst == L - W + m_src), jnp.logical_and(jnp.logical_and(m_src >= W, m_src < 2 * W), dst == m_src - W)), 1.0, 0.0).astype(BF16)
    q_to = iota((R, 2 * R), 0)
    q_at = iota((R, 2 * R), 1)
    settle = jnp.where(jnp.logical_or(jnp.logical_and(q_to < W, q_at == q_to + W), jnp.logical_and(q_to >= R - W, q_at == q_to + W)), 1.0, 0.0).astype(BF16)
    lane_c = iota((R, L), 1) // EW
    lane_m = iota((R, L), 1) % EW

    def dot(a, b):
        return jnp.dot(a, b, preferred_element_type=F32)

    tall = 3 - (f == 0).astype(jnp.int32) - (f == nf - 1).astype(jnp.int32)
    wide = 3 - (g == 0).astype(jnp.int32) - (g == ng - 1).astype(jnp.int32)
    pl.semaphore_wait(barrier, tall * wide - 1)

    sent = []

    def message(it, kind, d, src_ref, dst_ref):
        slot = (it * 4 + kind) * 8 + DIRS.index(d)
        return pltpu.make_async_remote_copy(
            src_ref=src_ref, dst_ref=dst_ref, send_sem=send_sem.at[slot], recv_sem=recv_sem.at[slot],
            device_id=where_to(d), device_id_type=MESH,
        )

    def send(copies):
        for d, copy in copies:
            pl.when(exists(d))(copy.start)
        sent.extend(copies)

    def receive(copies):
        for d, copy in copies:
            pl.when(exists(back(d)))(copy.wait_recv)

    loads[0].wait()
    for it in range(ITERS):
        for b in range(NB):
            cells = (u_in[b] if it == 0 else uslot[b]).reshape(C * R, L)
            cols = dot(cells, stap[b])
            rimc = jnp.zeros((R, L), F32)
            for c in range(C):
                part = cols[c * R : (c + 1) * R]
                ycols[b * R : (b + 1) * R, c * L : (c + 1) * L] = part[:, :L].astype(BF16)
                rimc = jnp.where(lane_c == c, part[:, L:], rimc)
            ycols[b * R : (b + 1) * R, LC:] = rimc.astype(BF16)
        smooth = dot(ptap[...], ycols[...])
        rim_own[it] = smooth[R:, :LC].astype(BF16)
        edge_own[it] = smooth[:, LC:].astype(BF16).reshape(2, R, L)
        xslot[...] = smooth[:R, :LC]
        msg_a = [(d, message(it, 0, d, rim_own.at[it], rim.at[it, ROW_SLOT[d[0]] - 1])) for d in ROWS]
        msg_a += [
            (d, message(it, 0, d, edge_own.at[it, 0 if d[0] == 0 else 1], edge.at[it, SIDE_SLOT[d[1]], ROW_SLOT[d[0]]]))
            for d in SIDES
        ]
        send(msg_a)

        if it == 0:
            loads[1].wait()
            for r in range(RB):
                turn[r] = vdat[0, 0, r].astype(BF16)
            loads[2].wait()
        for k in range(KB):
            parts[k] = lax.dot_general(
                turn[row_ids[0, 0, k]], ops[0, 0, k], (((1,), (1,)), ((), ())), preferred_element_type=F32
            )

        def tile_total(q):
            total = jnp.where(col_ids[0, 0, 0] == q, 1.0, 0.0) * parts[0]
            for k in range(1, KB):
                total = total + jnp.where(col_ids[0, 0, k] == q, 1.0, 0.0) * parts[k]
            return total

        for t in range(T1):
            tsum_own[it, 0, t] = tile_total(t).astype(BF16)
            tsum_own[it, 1, t] = tile_total(2 * T1 + t).astype(BF16)
        msg_b = [
            (d, message(it, 1, d, tsum_own.at[it, 0 if d[0] < 0 else 1], tsum.at[it, ROW_SLOT[d[0]] - 1])) for d in ROWS
        ]
        send(msg_b)
        totals = [tile_total(T1 + t) for t in range(T1)]

        receive(msg_a)
        rows_in = dot(settle, rim[it].reshape(2 * R, LC))
        came = [jnp.where(lane_m >= W, edge[it, 0, s].astype(F32), edge[it, 1, s].astype(F32)) for s in range(3)]
        corner = dot(settle, jnp.concatenate([came[1], came[2]], axis=0).astype(BF16))
        side = came[0] + corner
        spread = jnp.concatenate([jnp.where(lane_c == c, side, 0.0) for c in range(C)], axis=0).astype(BF16)
        side_in = dot(spread, place)
        receive(msg_b)
        totals = [totals[t] + (tsum[it, 0, t].astype(F32) + tsum[it, 1, t].astype(F32)) for t in range(T1)]
        lines = []
        for h in range(PIX // L):
            lines += swap_groups([t[:, h * L : (h + 1) * L] for t in totals])
        backward = jnp.swapaxes(jnp.stack(lines), 0, 1)

        extrap = []
        for c in range(C):
            here = slice(c * L, (c + 1) * L)
            old = image[c] if it == 0 else vslot[c]
            grad = backward[c] + (xslot[:, here] + rows_in[:, here] + side_in[c * R : (c + 1) * R])
            new = jnp.maximum(old - 0.5 * grad, 0.0)
            if it == ITERS - 1:
                image_out[c] = new
            else:
                vslot[c] = new
            ext = (2.0 * new - old).astype(BF16)
            near[it, 0, :, here] = ext
            extrap.append(ext)
        msg_c = [(d, message(it, 2, d, near.at[it, 0], near.at[it, ROW_SLOT[d[0]]])) for d in ROWS]
        flat = jnp.concatenate(extrap, axis=0)
        edges = dot(flat, pick)
        mine = jnp.zeros((R, L), F32)
        for c in range(C):
            mine = jnp.where(lane_c == c, edges[c * R : (c + 1) * R], mine)
        zedge_own[it] = mine.astype(BF16)
        msg_c += [
            (d, message(it, 2, d, zedge_own.at[it], zedge.at[it, SIDE_SLOT[d[1]], ROW_SLOT[d[0]]])) for d in SIDES
        ]
        send(msg_c)
        turned = jnp.swapaxes(flat.astype(F32).reshape(C, R, L), 0, 1)
        for h in range(PIX // L):
            tiles = swap_groups([turned[h * T1 + i] for i in range(T1)])
            for t in range(T1):
                ztile[it, T1 + t, :, h * L : (h + 1) * L] = tiles[t].astype(BF16)
        own_tiles = ztile.at[it, pl.ds(T1, T1)]
        msg_d = [
            (d, message(it, 3, d, own_tiles, ztile.at[it, pl.ds(2 * T1 if d[0] < 0 else 0, T1)])) for d in ROWS
        ]
        send(msg_d)

        receive(msg_c)
        zside = [jnp.where(lane_m >= W, zedge[it, 0, s].astype(F32), zedge[it, 1, s].astype(F32)) for s in range(3)]
        zside = jnp.concatenate(zside, axis=0).astype(BF16)
        side_rows = dot(rtap[...], zside)
        for c in range(C):
            lines_c = dot(rtap[...], near[it, :, :, c * L : (c + 1) * L].reshape(3 * R, L)).astype(BF16)
            side_c = jnp.where(iota((NB * R, L), 1) // EW == c, side_rows, 0.0).astype(BF16)
            rfilt[:, c, :, :L] = lines_c.reshape(NB, R, L)
            rfilt[:, c, :, L:] = side_c.reshape(NB, R, L)
        if it == 0:
            loads[4].wait()
        for b in range(NB):
            half = dot(rfilt[b].reshape(C * R, 2 * L), ttap[b]).reshape(C, R, L)
            cells = (u_in[b] if it == 0 else uslot[b]).astype(F32)
            widened = cells + half
            magnitude = jnp.sqrt(jnp.sum(widened * widened, axis=0))
            bound = thr[b]
            shrink = bound / jnp.maximum(magnitude, bound)
            new_u = (widened * shrink[None]).astype(BF16)
            if it == ITERS - 1:
                wave_out[b] = new_u
            else:
                uslot[b] = new_u

        receive(msg_d)
        for k in range(KB):
            parts[k] = dot(ztile[it, col_ids[0, 0, k]], ops[0, 0, k])
        if it == 0:
            loads[3].wait()
        for r in range(RB):
            pred = jnp.where(row_ids[0, 0, 0] == r, 1.0, 0.0) * parts[0]
            for k in range(1, KB):
                pred = pred + jnp.where(row_ids[0, 0, k] == r, 1.0, 0.0) * parts[k]
            moved = (vdat[0, 0, r] if it == 0 else data_out[0, 0, r]) + 0.5 * pred
            offset = 2.0 * moved - vis[0, 0, r]
            length = jnp.sqrt(jnp.sum(jnp.sum(offset * offset, axis=0, keepdims=True), axis=1, keepdims=True))
            ball = radius[0, 0, r]
            nearest = vis[0, 0, r] + offset * (ball / jnp.maximum(length, ball))
            new_v = moved - 0.5 * nearest
            data_out[0, 0, r] = new_v
            turn[r] = new_v.astype(BF16)

    for d, copy in sent:
        pl.when(exists(d))(copy.wait_send)


def solution(mesh):
    nf, ng = mesh.shape["facet"], mesh.shape["grp"]

    def per_device(image, dual_wave, thresholds, taps, seen, dual_data, radius, blocks, row_ids, col_ids):
        C, R, L = image.shape
        NB, _, TAPS = taps.shape
        KB, PIX, VB = blocks.shape[2:]
        RB = seen.shape[2]
        T1 = L // TS
        sizes = (nf, ng, NB, C, R, L, KB, RB, PIX, VB, TAPS, 3 * T1)
        vmem = pl.BlockSpec(memory_space=pltpu.VMEM)
        smem = pl.BlockSpec(memory_space=pltpu.SMEM)
        hbm = pl.BlockSpec(memory_space=pl.ANY)
        V = pltpu.VMEM
        messages = ITERS * 4 * 8
        return pl.pallas_call(
            functools.partial(kernel, sizes),
            out_shape=(
                jax.ShapeDtypeStruct(image.shape, F32),
                jax.ShapeDtypeStruct(dual_data.shape, F32),
                jax.ShapeDtypeStruct(dual_wave.shape, BF16),
            ),
            in_specs=[vmem, hbm, hbm, smem, hbm, hbm, smem, hbm, smem, smem],
            out_specs=(vmem, vmem, vmem),
            scratch_shapes=[
                V(dual_wave.shape, BF16),
                V(blocks.shape, BF16),
                V(thresholds.shape, F32),
                V(seen.shape, F32),
                V(dual_data.shape, F32),
                V((NB, 2 * L, L), BF16),
                V((NB, L, 2 * L), BF16),
                V((NB * R, 3 * R), BF16),
                V((2 * R, NB * R), BF16),
                V((NB * R, C * L + L), BF16),
                V((NB, C, R, 2 * L), BF16),
                V((ITERS, 3, R, C * L), BF16),
                V((8, 128), BF16),
                V((ITERS, 3 * T1, C, PIX), BF16),
                V((ITERS, 2, 3, R, L), BF16),
                V((ITERS, R, L), BF16),
                V((ITERS, R, C * L), BF16),
                V((ITERS, 2, R, C * L), BF16),
                V((ITERS, 2, R, L), BF16),
                V((ITERS, 2, 3, R, L), BF16),
                V((ITERS, 2, T1, C, PIX), BF16),
                V((ITERS, 2, T1, C, PIX), BF16),
                V((KB, C, max(PIX, VB)), F32),
                V(dual_wave.shape, BF16),
                V(image.shape, F32),
                V((R, C * L), F32),
                V((RB, C, VB), BF16),
                pltpu.SemaphoreType.DMA((5,)),
                pltpu.SemaphoreType.DMA((messages,)),
                pltpu.SemaphoreType.DMA((messages,)),
            ],
            compiler_params=pltpu.CompilerParams(collective_id=0, has_side_effects=True, vmem_limit_bytes=60 << 20),
        )(image, dual_wave, thresholds, taps, seen, dual_data, radius, blocks, row_ids, col_ids)

    dev = P("facet", "grp")
    rows = P(None, "facet", "grp")
    wave = P(None, None, "facet", "grp")
    return jax.shard_map(
        per_device,
        mesh=mesh,
        in_specs=(rows, wave, rows, P(), dev, dev, dev, dev, dev, dev),
        out_specs=(rows, dev, wave),
        check_vma=False,
    )
```

profile of v0, /device:TPU:1, one launch (start us, length us, event | category | flops | bytes accessed | tf_op | source)
XLA Modules:
  0.0 34.1 jit_solution(5323994727155505598)
XLA Ops:
  0.6 1.4 %copy.13.taps = f32[8,2,7]{2,1,0:T(2,128)} copy(f32[8,2,7]{0,1,2:T(2,128)} %param.13) | data formatting | bytes 896 | tf_op args[3]
  2.0 27.1 %shard_map.121 = (f32[16,16,128]{2,1,0:T(8,128)}, f32[1,1,8,16,256]{4,3,2,1,0:T(8,128)}, bf16[8,16,16,128]{3,2,1,0:T(8,128)(2,1)}) custom-call(f32[16,16,128]{2,1,0:T(8,128)} %image.1, bf16[8,16,16,128]{3,2,1,0:T(8,128)(2,1)} %dual_wave.1, f32[8,16,128]{2,1,0:T(8,128)} %thresholds.1, f32[8,2,7]{2,1,0:T(2,128)} %copy.13.taps, f32[1,1,8,16,256]{4,3,2,1,0:T(8,128)} %seen.1, ...), custom_call_target="tpu_custom_call" | custom-call | tf_op jit(solution)/shard_map/pallas_call | solution.py:318
  29.1 1.6 %copy.17 = f32[16,16,128]{2,1,0:T(8,128)} copy(f32[16,16,128]{2,1,0:T(8,128)} %get-tuple-element.6) | data formatting | bytes 262144
  30.7 1.6 %copy.18 = f32[1,1,8,16,256]{4,3,2,1,0:T(8,128)} copy(f32[1,1,8,16,256]{4,3,2,1,0:T(8,128)} %get-tuple-element.7) | data formatting | bytes 262144
  32.2 1.9 %copy.19 = bf16[8,16,16,128]{3,2,1,0:T(8,128)(2,1)} copy(bf16[8,16,16,128]{3,2,1,0:T(8,128)(2,1)} %get-tuple-element.8) | data formatting | bytes 1048576
where the time goes:
time: 34.4 us; the launch traced here: 34.1 us
  Pallas kernels  27.1 us (79%)
  local copies, waits for them, and re-layouts  6.38 us (19%)
  between operations  0.64 us (2%)
    pallas_call x1, Pallas kernels, per_device(): pl.pallas_call(functools.partial(kernel, sizes), out_shape=(jax.ShapeDtyp...  27.1 us
    unnamed x4, local copies, waits for them, and re-layouts  6.38 us

commit v1 on v0

--- a/solution.py
+++ b/solution.py
@@ -55,7 +55,7 @@
     image_out, data_out, wave_out,
     u_in, ops, thr, vis, vdat, ttap, stap, rtap, ptap, ycols, rfilt,
     near, zrim, ztile, zedge, zedge_own, rim_own, rim, edge_own, edge, tsum_own, tsum,
-    parts, uslot, vslot, xslot, turn,
+    parts, uslot, vslot, xslot, turn, links,
     local_sem, send_sem, recv_sem,
 ):
     nf, ng, NB, C, R, L, KB, RB, PIX, VB, TAPS, NT3 = sizes
@@ -105,8 +105,6 @@
     dst = iota((L, L), 1)
     m_dst = dst % EW
     m_src = src % EW
-    over = jnp.where(m_dst < W, m_dst - W, jnp.where(m_dst < 2 * W, L + m_dst - W, 4 * L))
-    halo = jnp.where(m_src < W, L + m_src, jnp.where(m_src < 2 * W, m_src - 2 * W, 4 * L))
     row_out = iota((2 * R, NB * R), 0)
     row_out = jnp.where(row_out < R, row_out, jnp.where(row_out < R + W, row_out - R - W, jnp.where(row_out < R + 2 * W, row_out - W, 4 * L)))
     row_in = iota((2 * R, NB * R), 1)
@@ -114,17 +112,57 @@
     row_at = jnp.where(row_at < R, row_at, jnp.where(row_at < 2 * R, row_at - 2 * R, row_at - R))
     row_to = iota((R, 3 * R), 0)
     synth_rows = jnp.zeros((2 * R, NB * R), F32)
+    sub, lane = iota((EW, L), 0), iota((EW, L), 1)
+    last_sub = sub + L - EW
+    m_lane = lane % EW
+    over_col = jnp.where(m_lane < W, m_lane - W, jnp.where(m_lane < 2 * W, L + m_lane - W, 4 * L))
+    halo_col = jnp.where(sub < W, L + sub, jnp.where(sub < 2 * W, sub - 2 * W, 4 * L))
+    none = jnp.zeros((EW, L), F32)
+
+    def band(values, sign):
+        ahead = (sign * (lane - sub) + W + L) % L
+        base = tap_matrix(ahead, values)
+        pieces = [base] + [pltpu.roll(base, n * EW, 1) for n in range(1, C)]
+        pieces[0] = jnp.where(lane < L // 2, base, 0.0)
+        pieces[-1] = jnp.where(lane < L // 2, 0.0, pieces[-1])
+        return pieces
+
+    def store(ref, b, row, col, pieces, low=False):
+        for n in range(0, len(pieces), 2):
+            value = jnp.concatenate(pieces[n : n + 2], axis=0)
+            high = value.astype(BF16)
+            ref[b, row + n * EW : row + (n + 2) * EW, col : col + L] = high
+            if low:
+                rest = (value - high.astype(F32)).astype(BF16)
+                ref[b, row + L + n * EW : row + L + (n + 2) * EW, col : col + L] = rest
+
     for b in range(NB):
-        rt = [taps[b, 0, t] for t in range(TAPS)]
-        ct = [taps[b, 1, t] for t in range(TAPS)]
+        rt = [taps[t, 0, b] for t in range(TAPS)]
+        ct = [taps[t, 1, b] for t in range(TAPS)]
         ch = [0.5 * t for t in ct]
-        stap[b, :, :L] = tap_matrix(dst + W - src, ct).astype(BF16)
-        stap[b, :, L:] = tap_matrix(over + W - src, ct).astype(BF16)
-        ttap[b, :L] = tap_matrix(src - dst + W, ch).astype(BF16)
-        ttap[b, L:] = tap_matrix(halo - dst + W, ch).astype(BF16)
+        store(stap, b, 0, 0, band(ct, 1), True)
+        rim_first = tap_matrix(over_col + W - sub, ct)
+        rim_last = tap_matrix(over_col + W - last_sub, ct)
+        store(stap, b, 0, L, [rim_first] + [none] * (C - 2) + [rim_last], True)
+        store(ttap, b, 0, 0, band(ch, -1))
+        store(ttap, b, L, 0, [tap_matrix(halo_col - lane + W, ch)] * C)
         rtap[b * R : (b + 1) * R] = tap_matrix(row_at - row_to + W, rt).astype(BF16)
         synth_rows = jnp.where(row_in // R == b, tap_matrix(row_out + W - (row_in - b * R), rt), synth_rows)
-    ptap[...] = synth_rows.astype(BF16)
+    rows_high = synth_rows.astype(BF16)
+    ptap[: 2 * R] = rows_high
+    ptap[2 * R :] = (synth_rows - rows_high.astype(F32)).astype(BF16)
+    for side, (ids, count) in enumerate(((col_ids, NT3), (row_ids, RB))):
+        for k in range(KB):
+            before = KB
+            for j in range(k):
+                before = jnp.where(ids[0, 0, j] == ids[0, 0, k], j, before)
+            links[2 * side, k] = before
+        for q in range(count):
+            last = KB
+            for k in range(KB):
+                last = jnp.where(ids[0, 0, k] == q, k, last)
+            links[2 * side + 1, q] = last
+    parts[KB] = jnp.zeros(parts.shape[1:], F32)
     pick = jnp.where(jnp.logical_or(jnp.logical_and(m_dst < W, src == m_dst), jnp.logical_and(jnp.logical_and(m_dst >= W, m_dst < 2 * W), src == L - 2 * W + m_dst)), 1.0, 0.0).astype(BF16)
     place = jnp.where(jnp.logical_or(jnp.logical_and(m_src < W, dst == L - W + m_src), jnp.logical_and(jnp.logical_and(m_src >= W, m_src < 2 * W), dst == m_src - W)), 1.0, 0.0).astype(BF16)
     q_to = iota((R, 2 * R), 0)
@@ -162,7 +200,7 @@
     for it in range(ITERS):
         for b in range(NB):
             cells = (u_in[b] if it == 0 else uslot[b]).reshape(C * R, L)
-            cols = dot(cells, stap[b])
+            cols = dot(jnp.concatenate([cells, cells], axis=1), stap[b])
             rimc = jnp.zeros((R, L), F32)
             for c in range(C):
                 part = cols[c * R : (c + 1) * R]
@@ -170,6 +208,7 @@
                 rimc = jnp.where(lane_c == c, part[:, L:], rimc)
             ycols[b * R : (b + 1) * R, LC:] = rimc.astype(BF16)
         smooth = dot(ptap[...], ycols[...])
+        smooth = smooth[: 2 * R] + smooth[2 * R :]
         rim_own[it] = smooth[R:, :LC].astype(BF16)
         edge_own[it] = smooth[:, LC:].astype(BF16).reshape(2, R, L)
         xslot[...] = smooth[:R, :LC]
@@ -186,15 +225,13 @@
                 turn[r] = vdat[0, 0, r].astype(BF16)
             loads[2].wait()
         for k in range(KB):
-            parts[k] = lax.dot_general(
+            part = lax.dot_general(
                 turn[row_ids[0, 0, k]], ops[0, 0, k], (((1,), (1,)), ((), ())), preferred_element_type=F32
             )
+            parts[k] = part + parts[links[0, k]] if k else part
 
         def tile_total(q):
-            total = jnp.where(col_ids[0, 0, 0] == q, 1.0, 0.0) * parts[0]
-            for k in range(1, KB):
-                total = total + jnp.where(col_ids[0, 0, k] == q, 1.0, 0.0) * parts[k]
-            return total
+            return parts[links[1, q]]
 
         for t in range(T1):
             tsum_own[it, 0, t] = tile_total(t).astype(BF16)
@@ -280,13 +317,12 @@
 
         receive(msg_d)
         for k in range(KB):
-            parts[k] = dot(ztile[it, col_ids[0, 0, k]], ops[0, 0, k])
+            part = dot(ztile[it, col_ids[0, 0, k]], ops[0, 0, k])
+            parts[k] = part + parts[links[2, k]] if k else part
         if it == 0:
             loads[3].wait()
         for r in range(RB):
-            pred = jnp.where(row_ids[0, 0, 0] == r, 1.0, 0.0) * parts[0]
-            for k in range(1, KB):
-                pred = pred + jnp.where(row_ids[0, 0, k] == r, 1.0, 0.0) * parts[k]
+            pred = parts[links[3, r]]
             moved = (vdat[0, 0, r] if it == 0 else data_out[0, 0, r]) + 0.5 * pred
             offset = 2.0 * moved - vis[0, 0, r]
             length = jnp.sqrt(jnp.sum(jnp.sum(offset * offset, axis=0, keepdims=True), axis=1, keepdims=True))
@@ -304,8 +340,9 @@
     nf, ng = mesh.shape["facet"], mesh.shape["grp"]
 
     def per_device(image, dual_wave, thresholds, taps, seen, dual_data, radius, blocks, row_ids, col_ids):
+        taps = jnp.transpose(taps, (2, 1, 0))
         C, R, L = image.shape
-        NB, _, TAPS = taps.shape
+        TAPS, _, NB = taps.shape
         KB, PIX, VB = blocks.shape[2:]
         RB = seen.shape[2]
         T1 = L // TS
@@ -331,9 +368,9 @@
                 V(seen.shape, F32),
                 V(dual_data.shape, F32),
                 V((NB, 2 * L, L), BF16),
-                V((NB, L, 2 * L), BF16),
+                V((NB, 2 * L, 2 * L), BF16),
                 V((NB * R, 3 * R), BF16),
-                V((2 * R, NB * R), BF16),
+                V((4 * R, NB * R), BF16),
                 V((NB * R, C * L + L), BF16),
                 V((NB, C, R, 2 * L), BF16),
                 V((ITERS, 3, R, C * L), BF16),
@@ -347,11 +384,12 @@
                 V((ITERS, 2, 3, R, L), BF16),
                 V((ITERS, 2, T1, C, PIX), BF16),
                 V((ITERS, 2, T1, C, PIX), BF16),
-                V((KB, C, max(PIX, VB)), F32),
+                V((KB + 1, C, max(PIX, VB)), F32),
                 V(dual_wave.shape, BF16),
                 V(image.shape, F32),
                 V((R, C * L), F32),
                 V((RB, C, VB), BF16),
+                pltpu.SMEM((4, max(KB, 3 * T1)), jnp.int32),
                 pltpu.SemaphoreType.DMA((5,)),
                 pltpu.SemaphoreType.DMA((messages,)),
                 pltpu.SemaphoreType.DMA((messages,)),

time: 34.4 us -> 32.9 us (0.956)
  local copies, waits for them, and re-layouts: 6.38 us -> 5.01 us
    unnamed x4 -> x3, local copies, waits for them, and re-layouts: 6.38 us -> 5.01 us
where the time goes in v1:
time: 32.9 us; the launch traced here: 32.7 us
  Pallas kernels  27.1 us (82%)
  local copies, waits for them, and re-layouts  5.01 us (15%)
  between operations  0.64 us (2%)
    pallas_call x1, Pallas kernels, per_device(): pl.pallas_call(functools.partial(kernel, sizes), out_shape=(jax.ShapeDtyp...  27.1 us
    unnamed x3, local copies, waits for them, and re-layouts  5.01 us

profile of v1, /device:TPU:1, one launch (start us, length us, event | category | flops | bytes accessed | tf_op | source)
XLA Modules:
  0.0 32.7 jit_solution(3418012299907436486)
XLA Ops:
  0.6 27.1 %shard_map.121 = (f32[16,16,128]{2,1,0:T(8,128)}, f32[1,1,8,16,256]{4,3,2,1,0:T(8,128)}, bf16[8,16,16,128]{3,2,1,0:T(8,128)(2,1)}) custom-call(f32[16,16,128]{2,1,0:T(8,128)} %image.1, bf16[8,16,16,128]{3,2,1,0:T(8,128)(2,1)} %dual_wave.1, f32[8,16,128]{2,1,0:T(8,128)} %thresholds.1, f32[7,2,8]{2,1,0:T(2,128)} %bitcast.1, f32[1,1,8,16,256]{4,3,2,1,0:T(8,128)} %seen.1, ...), custom_call_target="tpu_custom_call" | custom-call | tf_op jit(solution)/shard_map/pallas_call | solution.py:355
  27.7 1.6 %copy.16 = f32[16,16,128]{2,1,0:T(8,128)} copy(f32[16,16,128]{2,1,0:T(8,128)} %get-tuple-element.6) | data formatting | bytes 262144
  29.3 1.6 %copy.17 = f32[1,1,8,16,256]{4,3,2,1,0:T(8,128)} copy(f32[1,1,8,16,256]{4,3,2,1,0:T(8,128)} %get-tuple-element.7) | data formatting | bytes 262144
  30.8 1.9 %copy.18 = bf16[8,16,16,128]{3,2,1,0:T(8,128)(2,1)} copy(bf16[8,16,16,128]{3,2,1,0:T(8,128)(2,1)} %get-tuple-element.8) | data formatting | bytes 1048576

commit v2 on v1

--- a/solution.py
+++ b/solution.py
@@ -51,9 +51,9 @@
 
 def kernel(
     sizes,
-    image, dual_wave, thresholds, taps, seen, dual_data, radius, blocks, row_ids, col_ids,
+    image_hbm, dual_wave, thresholds, taps, seen, dual_data, radius, blocks, row_ids, col_ids,
     image_out, data_out, wave_out,
-    u_in, ops, thr, vis, vdat, ttap, stap, rtap, ptap, ycols, rfilt,
+    image, u_in, ops, thr, vis, vdat, ttap, stap, rtap, ptap, ycols, rfilt,
     near, zrim, ztile, zedge, zedge_own, rim_own, rim, edge_own, edge, tsum_own, tsum,
     parts, uslot, vslot, xslot, turn, links,
     local_sem, send_sem, recv_sem,
@@ -83,7 +83,7 @@
     loads = [
         pltpu.make_async_copy(src, dst, local_sem.at[n])
         for n, (src, dst) in enumerate(
-            ((dual_wave, u_in), (dual_data, vdat), (blocks, ops), (seen, vis), (thresholds, thr))
+            ((dual_wave, u_in), (dual_data, vdat), (blocks, ops), (seen, vis), (thresholds, thr), (image_hbm, image))
         )
     ]
     for load in loads:
@@ -256,6 +256,8 @@
             lines += swap_groups([t[:, h * L : (h + 1) * L] for t in totals])
         backward = jnp.swapaxes(jnp.stack(lines), 0, 1)
 
+        if it == 0:
+            loads[5].wait()
         extrap = []
         for c in range(C):
             here = slice(c * L, (c + 1) * L)
@@ -336,6 +338,34 @@
         pl.when(exists(d))(copy.wait_send)
 
 
+def hand_over(*refs):
+    count = (len(refs) - 2) // 3
+    sources, results, held = (refs[n * count : (n + 1) * count] for n in range(3))
+    in_sem, out_sem = refs[-2:]
+    into = [pltpu.make_async_copy(sources[n], held[n], in_sem.at[n]) for n in range(count)]
+    out = [pltpu.make_async_copy(held[n], results[n], out_sem.at[n]) for n in range(count)]
+    for copy in into:
+        copy.start()
+    for n in range(count):
+        into[n].wait()
+        out[n].start()
+    for copy in out:
+        copy.wait()
+
+
+def passed_on(arrays):
+    any_spec = pl.BlockSpec(memory_space=pl.ANY)
+    return pl.pallas_call(
+        hand_over,
+        out_shape=tuple(jax.ShapeDtypeStruct(a.shape, a.dtype) for a in arrays),
+        in_specs=[any_spec] * len(arrays),
+        out_specs=(any_spec,) * len(arrays),
+        scratch_shapes=[pltpu.VMEM(a.shape, a.dtype) for a in arrays]
+        + [pltpu.SemaphoreType.DMA((len(arrays),))] * 2,
+        compiler_params=pltpu.CompilerParams(vmem_limit_bytes=62 << 20),
+    )(*arrays)
+
+
 def solution(mesh):
     nf, ng = mesh.shape["facet"], mesh.shape["grp"]
 
@@ -349,19 +379,20 @@
         sizes = (nf, ng, NB, C, R, L, KB, RB, PIX, VB, TAPS, 3 * T1)
         vmem = pl.BlockSpec(memory_space=pltpu.VMEM)
         smem = pl.BlockSpec(memory_space=pltpu.SMEM)
-        hbm = pl.BlockSpec(memory_space=pl.ANY)
+        hbm = pl.BlockSpec(memory_space=pltpu.HBM)
         V = pltpu.VMEM
         messages = ITERS * 4 * 8
-        return pl.pallas_call(
+        results = pl.pallas_call(
             functools.partial(kernel, sizes),
             out_shape=(
                 jax.ShapeDtypeStruct(image.shape, F32),
                 jax.ShapeDtypeStruct(dual_data.shape, F32),
                 jax.ShapeDtypeStruct(dual_wave.shape, BF16),
             ),
-            in_specs=[vmem, hbm, hbm, smem, hbm, hbm, smem, hbm, smem, smem],
+            in_specs=[hbm, hbm, hbm, smem, hbm, hbm, smem, hbm, smem, smem],
             out_specs=(vmem, vmem, vmem),
             scratch_shapes=[
+                V(image.shape, F32),
                 V(dual_wave.shape, BF16),
                 V(blocks.shape, BF16),
                 V(thresholds.shape, F32),
@@ -390,12 +421,13 @@
                 V((R, C * L), F32),
                 V((RB, C, VB), BF16),
                 pltpu.SMEM((4, max(KB, 3 * T1)), jnp.int32),
-                pltpu.SemaphoreType.DMA((5,)),
+                pltpu.SemaphoreType.DMA((6,)),
                 pltpu.SemaphoreType.DMA((messages,)),
                 pltpu.SemaphoreType.DMA((messages,)),
             ],
             compiler_params=pltpu.CompilerParams(collective_id=0, has_side_effects=True, vmem_limit_bytes=60 << 20),
         )(image, dual_wave, thresholds, taps, seen, dual_data, radius, blocks, row_ids, col_ids)
+        return passed_on(results)
 
     dev = P("facet", "grp")
     rows = P(None, "facet", "grp")

time: 32.9 us -> 29.9 us (0.909)
  local copies, waits for them, and re-layouts: 5.01 us -> 0 us
  Pallas kernels: 27.1 us -> 29 us
    unnamed x3 -> x0, local copies, waits for them, and re-layouts: 5.01 us -> none
    pallas_call x0 -> x1, Pallas kernels: none -> 2.02 us  [passed_on(): pl.pallas_call(hand_over, out_shape=tuple((jax.ShapeDtypeStruct(a.shape,...]
where the time goes in v2:
time: 29.9 us; the launch traced here: 29.7 us
  Pallas kernels  29 us (97%)
  between operations  0.64 us (2%)
    pallas_call x1, Pallas kernels, per_device(): pl.pallas_call(functools.partial(kernel, sizes), out_shape=(jax.ShapeDtyp...  27 us
    pallas_call x1, Pallas kernels, passed_on(): pl.pallas_call(hand_over, out_shape=tuple((jax.ShapeDtypeStruct(a.shape,...  2.02 us

profile of v2, /device:TPU:1, one launch (start us, length us, event | category | flops | bytes accessed | tf_op | source)
XLA Modules:
  0.0 29.7 jit_solution(17847466286298078808)
XLA Ops:
  0.6 27.0 %shard_map.121 = (f32[16,16,128]{2,1,0:T(8,128)}, f32[1,1,8,16,256]{4,3,2,1,0:T(8,128)}, bf16[8,16,16,128]{3,2,1,0:T(8,128)(2,1)}) custom-call(f32[16,16,128]{2,1,0:T(8,128)} %image_hbm.1, bf16[8,16,16,128]{3,2,1,0:T(8,128)(2,1)} %dual_wave.1, f32[8,16,128]{2,1,0:T(8,128)} %thresholds.1, f32[7,2,8]{2,1,0:T(2,128)} %bitcast.1, f32[1,1,8,16,256]{4,3,2,1,0:T(8,128)} %seen.1, ...), custom_call_target="tpu_custom_call" | custom-call | tf_op jit(solution)/shard_map/pallas_call | solution.py:385
  27.6 2.0 %shard_map.122 = (f32[16,16,128]{2,1,0:T(8,128)}, f32[1,1,8,16,256]{4,3,2,1,0:T(8,128)}, bf16[8,16,16,128]{3,2,1,0:T(8,128)(2,1)}) custom-call(f32[16,16,128]{2,1,0:T(8,128)} %get-tuple-element.6.refs_0_, f32[1,1,8,16,256]{4,3,2,1,0:T(8,128)} %get-tuple-element.7.refs_1_, bf16[8,16,16,128]{3,2,1,0:T(8,128)(2,1)} %get-tuple-element.8.refs_2_), custom_call_target="tpu_custom_call" | custom-call | tf_op jit(solution)/shard_map/pallas_call | solution.py:358

commit v3 on v2

--- a/solution.py
+++ b/solution.py
@@ -196,8 +196,32 @@
         for d, copy in copies:
             pl.when(exists(back(d)))(copy.wait_recv)
 
-    loads[0].wait()
     for it in range(ITERS):
+        if it == 0:
+            loads[1].wait()
+            for r in range(RB):
+                turn[r] = vdat[0, 0, r].astype(BF16)
+            loads[2].wait()
+        for k in range(KB):
+            part = lax.dot_general(
+                turn[row_ids[0, 0, k]], ops[0, 0, k], (((1,), (1,)), ((), ())), preferred_element_type=F32
+            )
+            parts[k] = part + parts[links[0, k]] if k else part
+
+        def tile_total(q):
+            return parts[links[1, q]]
+
+        for t in range(T1):
+            tsum_own[it, 0, t] = tile_total(t).astype(BF16)
+            tsum_own[it, 1, t] = tile_total(2 * T1 + t).astype(BF16)
+        msg_b = [
+            (d, message(it, 1, d, tsum_own.at[it, 0 if d[0] < 0 else 1], tsum.at[it, ROW_SLOT[d[0]] - 1])) for d in ROWS
+        ]
+        send(msg_b)
+        totals = [tile_total(T1 + t) for t in range(T1)]
+
+        if it == 0:
+            loads[0].wait()
         for b in range(NB):
             cells = (u_in[b] if it == 0 else uslot[b]).reshape(C * R, L)
             cols = dot(jnp.concatenate([cells, cells], axis=1), stap[b])
@@ -219,28 +243,12 @@
         ]
         send(msg_a)
 
-        if it == 0:
-            loads[1].wait()
-            for r in range(RB):
-                turn[r] = vdat[0, 0, r].astype(BF16)
-            loads[2].wait()
-        for k in range(KB):
-            part = lax.dot_general(
-                turn[row_ids[0, 0, k]], ops[0, 0, k], (((1,), (1,)), ((), ())), preferred_element_type=F32
-            )
-            parts[k] = part + parts[links[0, k]] if k else part
-
-        def tile_total(q):
-            return parts[links[1, q]]
-
-        for t in range(T1):
-            tsum_own[it, 0, t] = tile_total(t).astype(BF16)
-            tsum_own[it, 1, t] = tile_total(2 * T1 + t).astype(BF16)
-        msg_b = [
-            (d, message(it, 1, d, tsum_own.at[it, 0 if d[0] < 0 else 1], tsum.at[it, ROW_SLOT[d[0]] - 1])) for d in ROWS
-        ]
-        send(msg_b)
-        totals = [tile_total(T1 + t) for t in range(T1)]
+        receive(msg_b)
+        totals = [totals[t] + (tsum[it, 0, t].astype(F32) + tsum[it, 1, t].astype(F32)) for t in range(T1)]
+        lines = []
+        for h in range(PIX // L):
+            lines += swap_groups([t[:, h * L : (h + 1) * L] for t in totals])
+        backward = jnp.swapaxes(jnp.stack(lines), 0, 1)
 
         receive(msg_a)
         rows_in = dot(settle, rim[it].reshape(2 * R, LC))
@@ -249,13 +257,6 @@
         side = came[0] + corner
         spread = jnp.concatenate([jnp.where(lane_c == c, side, 0.0) for c in range(C)], axis=0).astype(BF16)
         side_in = dot(spread, place)
-        receive(msg_b)
-        totals = [totals[t] + (tsum[it, 0, t].astype(F32) + tsum[it, 1, t].astype(F32)) for t in range(T1)]
-        lines = []
-        for h in range(PIX // L):
-            lines += swap_groups([t[:, h * L : (h + 1) * L] for t in totals])
-        backward = jnp.swapaxes(jnp.stack(lines), 0, 1)
-
         if it == 0:
             loads[5].wait()
         extrap = []
@@ -272,16 +273,17 @@
             near[it, 0, :, here] = ext
             extrap.append(ext)
         msg_c = [(d, message(it, 2, d, near.at[it, 0], near.at[it, ROW_SLOT[d[0]]])) for d in ROWS]
+        send(msg_c)
         flat = jnp.concatenate(extrap, axis=0)
         edges = dot(flat, pick)
         mine = jnp.zeros((R, L), F32)
         for c in range(C):
             mine = jnp.where(lane_c == c, edges[c * R : (c + 1) * R], mine)
         zedge_own[it] = mine.astype(BF16)
-        msg_c += [
+        msg_e = [
             (d, message(it, 2, d, zedge_own.at[it], zedge.at[it, SIDE_SLOT[d[1]], ROW_SLOT[d[0]]])) for d in SIDES
         ]
-        send(msg_c)
+        send(msg_e)
         turned = jnp.swapaxes(flat.astype(F32).reshape(C, R, L), 0, 1)
         for h in range(PIX // L):
             tiles = swap_groups([turned[h * T1 + i] for i in range(T1)])
@@ -294,6 +296,7 @@
         send(msg_d)
 
         receive(msg_c)
+        receive(msg_e)
         zside = [jnp.where(lane_m >= W, zedge[it, 0, s].astype(F32), zedge[it, 1, s].astype(F32)) for s in range(3)]
         zside = jnp.concatenate(zside, axis=0).astype(BF16)
         side_rows = dot(rtap[...], zside)

time: 29.9 us -> 30.4 us (1.017)
  the two profiles are of different devices: /device:TPU:1 before, /device:TPU:9 now
where the time goes in v3:
time: 30.4 us; the launch traced here: 30.2 us
  Pallas kernels  29.6 us (97%)
  between operations  0.64 us (2%)
    pallas_call x1, Pallas kernels, per_device(): pl.pallas_call(functools.partial(kernel, sizes), out_shape=(jax.ShapeDtyp...  27.5 us
    pallas_call x1, Pallas kernels, passed_on(): pl.pallas_call(hand_over, out_shape=tuple((jax.ShapeDtypeStruct(a.shape,...  2.02 us

profile of v3, /device:TPU:9, one launch (start us, length us, event | category | flops | bytes accessed | tf_op | source)
XLA Modules:
  0.0 30.2 jit_solution(9536806009828036759)
XLA Ops:
  0.6 27.5 %shard_map.121 = (f32[16,16,128]{2,1,0:T(8,128)}, f32[1,1,8,16,256]{4,3,2,1,0:T(8,128)}, bf16[8,16,16,128]{3,2,1,0:T(8,128)(2,1)}) custom-call(f32[16,16,128]{2,1,0:T(8,128)} %image_hbm.1, bf16[8,16,16,128]{3,2,1,0:T(8,128)(2,1)} %dual_wave.1, f32[8,16,128]{2,1,0:T(8,128)} %thresholds.1, f32[7,2,8]{2,1,0:T(2,128)} %bitcast.1, f32[1,1,8,16,256]{4,3,2,1,0:T(8,128)} %seen.1, ...), custom_call_target="tpu_custom_call" | custom-call | tf_op jit(solution)/shard_map/pallas_call | solution.py:388
  28.2 2.0 %shard_map.122 = (f32[16,16,128]{2,1,0:T(8,128)}, f32[1,1,8,16,256]{4,3,2,1,0:T(8,128)}, bf16[8,16,16,128]{3,2,1,0:T(8,128)(2,1)}) custom-call(f32[16,16,128]{2,1,0:T(8,128)} %get-tuple-element.6.refs_0_, f32[1,1,8,16,256]{4,3,2,1,0:T(8,128)} %get-tuple-element.7.refs_1_, bf16[8,16,16,128]{3,2,1,0:T(8,128)(2,1)} %get-tuple-element.8.refs_2_), custom_call_target="tpu_custom_call" | custom-call | tf_op jit(solution)/shard_map/pallas_call | solution.py:361
